TPU v7x, 32 devices: a whole 2x2x4 slice. The times are simulated.
32 devices in a mesh: rep: 2 (over x), walk: 16 (over z, y, core).
Axes of the slice: x: 2, y: 2, z: 4, core: 2. Of those that a mesh axis runs over, the one named last changes fastest.
Arguments:
- greens: bfloat16 [32, 64, 384], P(('rep', 'walk')), parts along dimension 0, may hold values from -6 to 6
- source: int32 [64], P(('rep', 'walk')), parts along dimension 0, may hold values from 0 to 15, as said below
- counts: int32 [32], P('rep'), parts along dimension 0, may hold values from 1 to 2, as said below
- cholesky: bfloat16 [512, 64, 384], P('walk'), may hold values from -0.0390625 to 0.0390625
Outputs:
- relocated: bfloat16 [64, 64, 384], P(('rep', 'walk')), parts along dimension 0
- exchange_energy: float32 [64], P(('rep', 'walk')), parts along dimension 0
- force_bias: float32 [64, 512], P(('rep', 'walk')), parts along dimension 0
There are 2 independent parts, one for each index of `rep`. A program takes and returns all parts, laid end to end along the dimension named above; an argument that names none is the same for every part. Nothing has to cross between parts.
Inputs may be any that keep to these rules, and one draw needn't show every extreme that they name: `source`: slot s belongs to walk device s div 2. Its walker comes from that device or one of the two devices beside it along the closed loop of walk devices. Slots beyond a device's count also name some walker. Slots 0 to counts[d] - 1 of device d are live.
All inputs are finite; a program needn't handle non-finite values.
Results may differ from a plain program's by a relative error of at most 0.001.
Values may be sent and summed in bfloat16 or wider, within the bound.
A program may use at most 64 MiB of HBM per device.

v0:
```python
import jax
import jax.numpy as jnp
from jax import lax
from jax.sharding import PartitionSpec as P


def padded(block, sides, width):
    for axis, dim in sides:
        count = lax.axis_size(axis)
        forward = [(i, i + 1) for i in range(count - 1)]
        forward.append((count - 1, 0))
        backward = [(target, source) for source, target in forward]
        low = lax.ppermute(
            lax.slice_in_dim(block, block.shape[dim] - width, None, axis=dim), axis, forward
        )
        high = lax.ppermute(lax.slice_in_dim(block, 0, width, axis=dim), axis, backward)
        block = jnp.concatenate([low, block, high], axis=dim)
    return block


def body(greens, source, counts, cholesky):
    walkers = lax.axis_size("walk")
    my_index = lax.axis_index("walk")
    old_slots = greens.shape[0]
    new_slots = source.shape[0]
    chol_dev = cholesky.shape[0]
    occupied = cholesky.shape[1]
    orbitals = cholesky.shape[2]
    nchol = chol_dev * walkers
    nearby = padded(greens, (("walk", 0),), old_slots)
    src_dev = source // old_slots
    relative = (src_dev - my_index + 1) % walkers
    chosen = relative * old_slots + source % old_slots
    my_count = lax.dynamic_index_in_dim(counts, my_index, 0, keepdims=False)
    is_live = jnp.arange(new_slots) < my_count
    relocated = jnp.where(
        is_live[:, None, None], jnp.take(nearby, chosen, axis=0), jnp.zeros((), jnp.bfloat16)
    )
    chol_rows = cholesky.reshape(chol_dev, occupied * orbitals)
    batch_dims = (((2,), (2,)), ((0,), (0,)))

    def group_energy(group_in):
        members = group_in.shape[0]
        spread = jnp.broadcast_to(
            group_in[:, None], (members, chol_dev, occupied, orbitals)
        ).reshape(members * chol_dev, occupied, orbitals)
        stacked = jnp.broadcast_to(cholesky[None], (members, chol_dev, occupied, orbitals)).reshape(
            members * chol_dev, occupied, orbitals
        )
        forward = lax.dot_general(stacked, spread, batch_dims, preferred_element_type=jnp.float32)
        mirrored = lax.dot_general(spread, stacked, batch_dims, preferred_element_type=jnp.float32)
        return -(0.5 / nchol) * jnp.sum((forward * mirrored).reshape(members, -1), axis=1)

    block_in = lax.all_gather(greens, "walk", axis=0, tiled=True)
    total_rows = block_in.shape[0]
    group = 1
    for candidate in range(1, 5):
        if total_rows % candidate == 0:
            group = candidate
    grouped = block_in.reshape(total_rows // group, group, occupied, orbitals)
    energies = lax.map(group_energy, grouped).reshape(total_rows)
    biases = lax.dot_general(
        block_in.reshape(block_in.shape[0], occupied * orbitals),
        chol_rows,
        (((1,), (1,)), ((), ())),
        preferred_element_type=jnp.float32,
    )
    bias_mine, energy_cols = (
        lax.all_to_all(biases, "walk", split_axis=0, concat_axis=1, tiled=True),
        lax.all_to_all(energies[:, None], "walk", split_axis=0, concat_axis=1, tiled=True),
    )
    energy_mine = jnp.sum(energy_cols, axis=1)
    bias_near, energy_near = (
        padded(bias_mine, (("walk", 0),), old_slots),
        padded(energy_mine, (("walk", 0),), old_slots),
    )
    bias_rows = jnp.take(bias_near, chosen, axis=0)
    energy_slot = jnp.take(energy_near, chosen, axis=0)
    exchange_energy = jnp.where(is_live, energy_slot, 0.0)
    force_bias = jnp.where(is_live[:, None], bias_rows, 0.0)
    return (relocated, exchange_energy, force_bias)


def solution(mesh):
    return jax.shard_map(
        body,
        mesh=mesh,
        in_specs=(
            P(("rep", "walk"), None, None),
            P(("rep", "walk")),
            P("rep"),
            P("walk", None, None),
        ),
        out_specs=(P(("rep", "walk"), None, None), P(("rep", "walk")), P(("rep", "walk"), None)),
        check_vma=False,
    )
```

profile of v0, /device:TPU:0, one launch (start us, length us, event | category | flops | bytes accessed | tf_op | source)
XLA Modules:
  0.0 130.4 jit_solution(3880565610310121807)
XLA Ops:
  0.6 0.5 collective-permute-start
  1.1 5.1 %collective-permute-start.1 = (bf16[1,64,384]{2,1,0:T(8,128)(2,1)}, bf16[1,64,384]{2,1,0:T(8,128)(2,1)S(1)}, u32[]{:S(2)}, u32[]{:S(2)}) collective-permute-start(bf16[1,64,384]{2,1,0:T(8,128)(2,1)} %param.6), channel_id=1, source_target_pairs={{1,0},{2,1},{3,2},{4,3},{5,4},{6,5},{7,6},{8,7},{9,8},{10,9},{11,1... | collective-permute-start | bytes 147464 | tf_op jit(solution)/shard_map/ppermute | solution.py:16
  6.2 21.7 %all_gather.3 = bf16[16,64,384]{2,1,0:T(8,128)(2,1)S(1)} all-gather(bf16[1,64,384]{2,1,0:T(8,128)(2,1)} %param.6), channel_id=1, replica_groups=mesh['rep'=2,'walk'=16] {'walk'}, dimensions={0}, use_global_device_ids=true | all-gather | bytes 835584 | tf_op jit(solution)/shard_map/all_gather | solution.py:54
  27.9 68.6 %while.10 = (s32[]{:T(128)}, f32[4,4]{1,0:T(4,128)S(1)}, bf16[4,4,64,384]{3,2,1,0:T(8,128)(2,1)S(1)}, bf16[32,64,384]{2,1,0:T(8,128)(2,1)}, s32[]{:T(128)}, /*index=5*/f32[]{:T(128)}, s32[]{:T(128)}) while((s32[]{:T(128)}, f32[4,4]{1,0:T(4,128)S(1)}, bf16[4,4,64,384]{3,2,1,0:T(8,128)(2,1)S(1)}, bf16[32,64,384]{2,1,0:T(8,128)(2,1)}, s32[]{:T(128)}, ...), condition=%wide.region_3.4_spmd, body=%wide.region_0.3_spmd.sunk | while | flops 403701760 | bytes 44107972 | solution.py:61
  28.0 1.0 broadcast_in_dim.91
  29.0 0.4 copy-done
  29.4 1.0 broadcast_in_dim.92
  30.4 4.3 %fusion.14 = f32[128,64,64]{2,1,0:T(8,128)} fusion(bf16[128,64,384]{2,1,0:T(8,128)(2,1)S(1)} %bitcast.33, bf16[128,64,384]{2,1,0:T(8,128)(2,1)S(1)} %bitcast.34), kind=kOutput, calls=%fused_computation.24.clone.1 | convolution fusion | flops 402653184 | bytes 14680064 | tf_op jit(solution)/shard_map/while/body/eval_jaxpr/dot_general | solution.py:50
  34.7 5.7 %copy.25 = f32[128,64,64]{1,2,0:T(8,128)} copy(f32[128,64,64]{2,1,0:T(8,128)} %fusion.14) | data formatting | bytes 4194304 | tf_op jit(solution)/shard_map/while/body/eval_jaxpr/dot_general | solution.py:50
  40.3 4.5 %fusion.15 = f32[128]{0:T(128)S(1)} fusion(f32[128,64,64]{2,1,0:T(8,128)} %fusion.14, f32[128,64,64]{1,2,0:T(8,128)} %copy.25), kind=kLoop, calls=%fused_computation.4.clone.1 | loop fusion | flops 1048448 | bytes 4194816 | tf_op jit(solution)/shard_map/while/body/eval_jaxpr/reduce_sum | solution.py:52
  45.1 1.0 broadcast_in_dim.91
  46.2 0.3 copy-done
  46.5 1.0 broadcast_in_dim.92
  47.6 4.3 %fusion.14 = f32[128,64,64]{2,1,0:T(8,128)} fusion(bf16[128,64,384]{2,1,0:T(8,128)(2,1)S(1)} %bitcast.33, bf16[128,64,384]{2,1,0:T(8,128)(2,1)S(1)} %bitcast.34), kind=kOutput, calls=%fused_computation.24.clone.1 | convolution fusion | flops 402653184 | bytes 14680064 | tf_op jit(solution)/shard_map/while/body/eval_jaxpr/dot_general | solution.py:50
  51.8 5.7 %copy.25 = f32[128,64,64]{1,2,0:T(8,128)} copy(f32[128,64,64]{2,1,0:T(8,128)} %fusion.14) | data formatting | bytes 4194304 | tf_op jit(solution)/shard_map/while/body/eval_jaxpr/dot_general | solution.py:50
  57.5 4.5 %fusion.15 = f32[128]{0:T(128)S(1)} fusion(f32[128,64,64]{2,1,0:T(8,128)} %fusion.14, f32[128,64,64]{1,2,0:T(8,128)} %copy.25), kind=kLoop, calls=%fused_computation.4.clone.1 | loop fusion | flops 1048448 | bytes 4194816 | tf_op jit(solution)/shard_map/while/body/eval_jaxpr/reduce_sum | solution.py:52
  62.3 1.0 broadcast_in_dim.91
  63.3 0.3 copy-done
  63.7 1.0 broadcast_in_dim.92
  64.7 4.3 %fusion.14 = f32[128,64,64]{2,1,0:T(8,128)} fusion(bf16[128,64,384]{2,1,0:T(8,128)(2,1)S(1)} %bitcast.33, bf16[128,64,384]{2,1,0:T(8,128)(2,1)S(1)} %bitcast.34), kind=kOutput, calls=%fused_computation.24.clone.1 | convolution fusion | flops 402653184 | bytes 14680064 | tf_op jit(solution)/shard_map/while/body/eval_jaxpr/dot_general | solution.py:50
  69.0 5.7 %copy.25 = f32[128,64,64]{1,2,0:T(8,128)} copy(f32[128,64,64]{2,1,0:T(8,128)} %fusion.14) | data formatting | bytes 4194304 | tf_op jit(solution)/shard_map/while/body/eval_jaxpr/dot_general | solution.py:50
  74.6 4.5 %fusion.15 = f32[128]{0:T(128)S(1)} fusion(f32[128,64,64]{2,1,0:T(8,128)} %fusion.14, f32[128,64,64]{1,2,0:T(8,128)} %copy.25), kind=kLoop, calls=%fused_computation.4.clone.1 | loop fusion | flops 1048448 | bytes 4194816 | tf_op jit(solution)/shard_map/while/body/eval_jaxpr/reduce_sum | solution.py:52
  79.4 1.0 broadcast_in_dim.91
  80.8 1.0 broadcast_in_dim.92
  81.8 4.3 %fusion.14 = f32[128,64,64]{2,1,0:T(8,128)} fusion(bf16[128,64,384]{2,1,0:T(8,128)(2,1)S(1)} %bitcast.33, bf16[128,64,384]{2,1,0:T(8,128)(2,1)S(1)} %bitcast.34), kind=kOutput, calls=%fused_computation.24.clone.1 | convolution fusion | flops 402653184 | bytes 14680064 | tf_op jit(solution)/shard_map/while/body/eval_jaxpr/dot_general | solution.py:50
  86.1 5.7 %copy.25 = f32[128,64,64]{1,2,0:T(8,128)} copy(f32[128,64,64]{2,1,0:T(8,128)} %fusion.14) | data formatting | bytes 4194304 | tf_op jit(solution)/shard_map/while/body/eval_jaxpr/dot_general | solution.py:50
  91.8 4.5 %fusion.15 = f32[128]{0:T(128)S(1)} fusion(f32[128,64,64]{2,1,0:T(8,128)} %fusion.14, f32[128,64,64]{1,2,0:T(8,128)} %copy.25), kind=kLoop, calls=%fused_computation.4.clone.1 | loop fusion | flops 1048448 | bytes 4194816 | tf_op jit(solution)/shard_map/while/body/eval_jaxpr/reduce_sum | solution.py:52
  96.5 0.7 all_to_all.27
  97.2 3.5 %all-to-all-start = ((f32[16,1,1]{2,1,0:T(1,128)}), f32[16,1,1]{2,1,0:T(1,128)S(1)}, u32[]{:S(2)}, u32[]{:S(2)}) async-start(f32[16,1,1]{2,1,0:T(1,128)} %all_to_all.27), calls=%async_computation | async-start | bytes 16384 | tf_op jit(solution)/shard_map/all_to_all | solution.py:70
  100.7 3.7 %fusion.1 = f32[16,32,1]{1,0,2:T(8,128)} fusion(bf16[32,64,384]{2,1,0:T(8,128)(2,1)} %get-tuple-element.91, bf16[16,64,384]{2,1,0:T(8,128)(2,1)S(1)} %bitcast.36), kind=kOutput, calls=%fused_computation.7 | convolution fusion | flops 25165824 | bytes 2361344 | tf_op jit(solution)/shard_map/dot_general | solution.py:62
  104.4 0.6 dynamic_slice.8
  105.0 0.7 compare_and_fusion
  105.7 1.3 all-to-all-done
  107.0 4.7 %all-to-all-start.1 = ((f32[16,1,32]{2,1,0:T(1,128)}), f32[16,1,32]{2,1,0:T(1,128)S(1)}, u32[]{:S(2)}, u32[]{:S(2)}) async-start(f32[16,1,32]{2,1,0:T(1,128)} %bitcast.10), calls=%async_computation.1 | async-start | bytes 16384 | tf_op jit(solution)/shard_map/all_to_all | solution.py:69
  111.7 0.6 reduce_sum.25
  112.3 0.4 collective-permute-start.2
  112.7 4.0 %collective-permute-start.3 = (f32[1]{0:T(128)}, f32[1]{0:T(128)}, u32[]{:S(2)}, u32[]{:S(2)}) collective-permute-start(f32[1]{0:T(128)} %bitcast.7), channel_id=1, source_target_pairs={{1,0},{2,1},{3,2},{4,3},{5,4},{6,5},{7,6},{8,7},{9,8},{10,9},{11,1... | collective-permute-start | bytes 20 | tf_op jit(solution)/shard_map/ppermute | solution.py:16
  116.8 1.3 %collective-permute-done.2 = f32[1]{0:T(128)} collective-permute-done((f32[1]{0:T(128)}, f32[1]{0:T(128)}, u32[]{:S(2)}, u32[]{:S(2)}) %collective-permute-start.2) | collective-permute-done | bytes 36 | tf_op jit(solution)/shard_map/ppermute | solution.py:13
  118.2 2.0 %pad_maximum_fusion.2 = f32[3]{0:T(128)S(1)} fusion(f32[1]{0:T(128)} %collective-permute-done.3, f32[1]{0:T(128)} %bitcast.7, f32[1]{0:T(128)} %collective-permute-done.2), kind=kLoop, calls=%fused_computation.21 | loop fusion | flops 6 | bytes 24 | tf_op jit(solution)/shard_map/concatenate | solution.py:17
  120.2 0.6 gather_fusion.1
  120.8 0.5 broadcast.101
  121.3 0.7 reduce.8
  122.1 4.4 %collective-permute-start.5 = (f32[1,512]{1,0:T(1,128)S(1)}, f32[1,512]{1,0:T(1,128)S(1)}, u32[]{:S(2)}, u32[]{:S(2)}) collective-permute-start(f32[1,512]{1,0:T(1,128)S(1)} %all_to_all.26), channel_id=1, source_target_pairs={{1,0},{2,1},{3,2},{4,3},{5,4},{6,5},{7,6},{8,7},{9,8},{10,9},{11,1... | collective-permute-start | bytes 6152 | tf_op jit(solution)/shard_map/ppermute | solution.py:16
  126.5 1.2 select_select_fusion.2
  127.8 0.6 gather_fusion.2
  128.4 0.7 select_select_fusion.1
  129.1 0.6 gather_fusion
  129.7 0.7 select_select_fusion
  (43 shorter events, 1.9 us)
Async XLA Ops:
  0.6 128.4 %collective-permute-start = (bf16[1,64,384]{2,1,0:T(8,128)(2,1)}, bf16[1,64,384]{2,1,0:T(8,128)(2,1)S(1)}, u32[]{:S(2)}, u32[]{:S(2)}) collective-permute-start(bf16[1,64,384]{2,1,0:T(8,128)(2,1)} %param.6), channel_id=1, source_target_pairs={{0,1},{1,2},{2,3},{3,4},{4,5},{5,6},{6,7},{7,8},{8,9},{9,10},{10,1... | collective-permute-start | bytes 147464 | tf_op jit(solution)/shard_map/ppermute | solution.py:13
  1.1 127.9 %collective-permute-start.1 = (bf16[1,64,384]{2,1,0:T(8,128)(2,1)}, bf16[1,64,384]{2,1,0:T(8,128)(2,1)S(1)}, u32[]{:S(2)}, u32[]{:S(2)}) collective-permute-start(bf16[1,64,384]{2,1,0:T(8,128)(2,1)} %param.6), channel_id=1, source_target_pairs={{1,0},{2,1},{3,2},{4,3},{5,4},{6,5},{7,6},{8,7},{9,8},{10,9},{11,1... | collective-permute-start | bytes 147464 | tf_op jit(solution)/shard_map/ppermute | solution.py:16
  27.9 76.5 %copy-start.3 = (s32[16]{0:T(128)S(1)}, s32[16]{0:T(128)}, u32[]{:S(2)}) copy-start(s32[16]{0:T(128)} %param.8) | copy-start | bytes 196
  27.9 77.1 %copy-start.2 = (s32[2]{0:T(128)S(1)}, s32[2]{0:T(128)}, u32[]{:S(2)}) copy-start(s32[2]{0:T(128)} %param.7) | copy-start | bytes 28
  27.9 101.2 %copy-start.1 = (bf16[1,64,384]{2,1,0:T(8,128)(2,1)S(1)}, bf16[1,64,384]{2,1,0:T(8,128)(2,1)}, u32[]{:S(2)}) copy-start(bf16[1,64,384]{2,1,0:T(8,128)(2,1)} %param.6) | copy-start | bytes 147460
  27.9 1.4 %copy-start = (bf16[32,64,384]{2,1,0:T(8,128)(2,1)S(1)}, bf16[32,64,384]{2,1,0:T(8,128)(2,1)}, u32[]{:S(2)}) copy-start(bf16[32,64,384]{2,1,0:T(8,128)(2,1)} %get-tuple-element.87) | copy-start | bytes 4718596 | tf_op jit(solution)/shard_map/while
  45.1 1.4 %copy-start = (bf16[32,64,384]{2,1,0:T(8,128)(2,1)S(1)}, bf16[32,64,384]{2,1,0:T(8,128)(2,1)}, u32[]{:S(2)}) copy-start(bf16[32,64,384]{2,1,0:T(8,128)(2,1)} %get-tuple-element.87) | copy-start | bytes 4718596 | tf_op jit(solution)/shard_map/while
  62.2 1.4 %copy-start = (bf16[32,64,384]{2,1,0:T(8,128)(2,1)S(1)}, bf16[32,64,384]{2,1,0:T(8,128)(2,1)}, u32[]{:S(2)}) copy-start(bf16[32,64,384]{2,1,0:T(8,128)(2,1)} %get-tuple-element.87) | copy-start | bytes 4718596 | tf_op jit(solution)/shard_map/while
  79.4 1.4 %copy-start = (bf16[32,64,384]{2,1,0:T(8,128)(2,1)S(1)}, bf16[32,64,384]{2,1,0:T(8,128)(2,1)}, u32[]{:S(2)}) copy-start(bf16[32,64,384]{2,1,0:T(8,128)(2,1)} %get-tuple-element.87) | copy-start | bytes 4718596 | tf_op jit(solution)/shard_map/while
  97.2 9.8 %all-to-all-start = ((f32[16,1,1]{2,1,0:T(1,128)}), f32[16,1,1]{2,1,0:T(1,128)S(1)}, u32[]{:S(2)}, u32[]{:S(2)}) async-start(f32[16,1,1]{2,1,0:T(1,128)} %all_to_all.27), calls=%async_computation | async-start | bytes 16384 | tf_op jit(solution)/shard_map/all_to_all | solution.py:70
  107.0 13.8 %all-to-all-start.1 = ((f32[16,1,32]{2,1,0:T(1,128)}), f32[16,1,32]{2,1,0:T(1,128)S(1)}, u32[]{:S(2)}, u32[]{:S(2)}) async-start(f32[16,1,32]{2,1,0:T(1,128)} %bitcast.10), calls=%async_computation.1 | async-start | bytes 16384 | tf_op jit(solution)/shard_map/all_to_all | solution.py:69
  112.3 5.7 %collective-permute-start.2 = (f32[1]{0:T(128)}, f32[1]{0:T(128)}, u32[]{:S(2)}, u32[]{:S(2)}) collective-permute-start(f32[1]{0:T(128)} %bitcast.7), channel_id=1, source_target_pairs={{0,1},{1,2},{2,3},{3,4},{4,5},{5,6},{6,7},{7,8},{8,9},{9,10},{10,1... | collective-permute-start | bytes 20 | tf_op jit(solution)/shard_map/ppermute | solution.py:13
  112.7 5.5 %collective-permute-start.3 = (f32[1]{0:T(128)}, f32[1]{0:T(128)}, u32[]{:S(2)}, u32[]{:S(2)}) collective-permute-start(f32[1]{0:T(128)} %bitcast.7), channel_id=1, source_target_pairs={{1,0},{2,1},{3,2},{4,3},{5,4},{6,5},{7,6},{8,7},{9,8},{10,9},{11,1... | collective-permute-start | bytes 20 | tf_op jit(solution)/shard_map/ppermute | solution.py:16
  122.1 5.7 %collective-permute-start.4 = (f32[1,512]{1,0:T(1,128)S(1)}, f32[1,512]{1,0:T(1,128)S(1)}, u32[]{:S(2)}, u32[]{:S(2)}) collective-permute-start(f32[1,512]{1,0:T(1,128)S(1)} %all_to_all.26), channel_id=1, source_target_pairs={{0,1},{1,2},{2,3},{3,4},{4,5},{5,6},{6,7},{7,8},{8,9},{9,10},{10,1... | collective-permute-start | bytes 6152 | tf_op jit(solution)/shard_map/ppermute | solution.py:13
  122.1 5.7 %collective-permute-start.5 = (f32[1,512]{1,0:T(1,128)S(1)}, f32[1,512]{1,0:T(1,128)S(1)}, u32[]{:S(2)}, u32[]{:S(2)}) collective-permute-start(f32[1,512]{1,0:T(1,128)S(1)} %all_to_all.26), channel_id=1, source_target_pairs={{1,0},{2,1},{3,2},{4,3},{5,4},{6,5},{7,6},{8,7},{9,8},{10,9},{11,1... | collective-permute-start | bytes 6152 | tf_op jit(solution)/shard_map/ppermute | solution.py:16
where the time goes:
time: 131 us; the launch traced here: 130 us
  local copies, waits for them, and re-layouts  36.5 us (28%)
  other arithmetic  25 us (19%)
  starting transfers between devices  22.6 us (17%)
  blocking collectives  21.7 us (17%)
  matrix products  20.8 us (16%)
  waiting for transfers between devices  2.86 us (2%)
    dot_general x4, local copies, waits for them, and re-layouts, group_energy(): lax.dot_general(stacked, spread, batch_dims, preferred_element_type=jnp.f...  22.6 us
    all_gather x1, blocking collectives, body(): block_in = lax.all_gather(greens, 'walk', axis=0, tiled=True)  21.7 us
    reduce_sum x8, other arithmetic, group_energy(): jnp.sum((forward * mirrored).reshape(members, -1), axis=1)  18.5 us
    dot_general x4, matrix products, group_energy(): lax.dot_general(stacked, spread, batch_dims, preferred_element_type=jnp.f...  17.1 us
    ppermute x3, starting transfers between devices, padded(): lax.ppermute(lax.slice_in_dim(block, 0, width, axis=dim), axis, backward)  13.5 us
    all_to_all x1, starting transfers between devices, body(): lax.all_to_all(biases, 'walk', split_axis=0, concat_axis=1, tiled=True)  4.71 us
    broadcast_in_dim x8, local copies, waits for them, and re-layouts, group_energy(): jnp.broadcast_to(group_in[:, None], (members, chol_dev, occupied, orbitals))  4.26 us
    broadcast_in_dim x4, local copies, waits for them, and re-layouts, group_energy(): jnp.broadcast_to(cholesky[None], (members, chol_dev, occupied, orbitals))  4.15 us
  transfers between devices with their start and end apart: 8, of which 4 were waited for; matrix products, arithmetic and copies ran while one was open for 61% of the time, Pallas kernels for 0%

commit v1 on v0

--- a/solution.py
+++ b/solution.py
@@ -67,7 +67,12 @@
     )
     bias_mine, energy_cols = (
         lax.all_to_all(biases, "walk", split_axis=0, concat_axis=1, tiled=True),
-        lax.all_to_all(energies[:, None], "walk", split_axis=0, concat_axis=1, tiled=True),
+        jnp.concatenate(
+            jax.lax.all_to_all(
+                jnp.stack(jnp.split(energies[:, None], jax.lax.axis_size("walk"), 0)), "walk", 0, 0
+            ),
+            1,
+        ),
     )
     energy_mine = jnp.sum(energy_cols, axis=1)
     bias_near, energy_near = (

time: 131 us -> 150 us (1.15)
  local copies, waits for them, and re-layouts: 36.5 us -> 54.8 us
    unnamed x6 -> x21, local copies, waits for them, and re-layouts: 0.01 us -> 17 us
  transfers between devices with their start and end apart: 8 -> 8, of which waited for: 4 -> 4; matrix products, arithmetic and copies ran while one was open for 61% -> 66% of each run, Pallas kernels for 0% -> 0%
where the time goes in v1:
time: 150 us; the launch traced here: 149 us
  local copies, waits for them, and re-layouts  54.8 us (37%)
  other arithmetic  25 us (17%)
  starting transfers between devices  22.7 us (15%)
  blocking collectives  21.7 us (14%)
  matrix products  20.8 us (14%)
  waiting for transfers between devices  2.9 us (2%)
    dot_general x4, local copies, waits for them, and re-layouts, group_energy(): lax.dot_general(stacked, spread, batch_dims, preferred_element_type=jnp.f...  22.7 us
    all_gather x1, blocking collectives, body(): block_in = lax.all_gather(greens, 'walk', axis=0, tiled=True)  21.7 us
    reduce_sum x8, other arithmetic, group_energy(): jnp.sum((forward * mirrored).reshape(members, -1), axis=1)  18.5 us
    dot_general x4, matrix products, group_energy(): lax.dot_general(stacked, spread, batch_dims, preferred_element_type=jnp.f...  17.1 us
    unnamed x21, local copies, waits for them, and re-layouts  17 us
    ppermute x3, starting transfers between devices, padded(): lax.ppermute(lax.slice_in_dim(block, 0, width, axis=dim), axis, backward)  13.6 us
    all_to_all x1, starting transfers between devices, body(): lax.all_to_all(biases, 'walk', split_axis=0, concat_axis=1, tiled=True)  4.71 us
    broadcast_in_dim x8, local copies, waits for them, and re-layouts, group_energy(): jnp.broadcast_to(group_in[:, None], (members, chol_dev, occupied, orbitals))  4.26 us
  transfers between devices with their start and end apart: 8, of which 4 were waited for; matrix products, arithmetic and copies ran while one was open for 66% of the time, Pallas kernels for 0%

profile of v1, /device:TPU:0, one launch (start us, length us, event | category | flops | bytes accessed | tf_op | source)
XLA Modules:
  0.0 148.8 jit_solution(3029773397947720061)
XLA Ops:
  1.1 5.1 %collective-permute-start.1 = (bf16[1,64,384]{2,1,0:T(8,128)(2,1)}, bf16[1,64,384]{2,1,0:T(8,128)(2,1)S(1)}, u32[]{:S(2)}, u32[]{:S(2)}) collective-permute-start(bf16[1,64,384]{2,1,0:T(8,128)(2,1)} %param.6), channel_id=1, source_target_pairs={{1,0},{2,1},{3,2},{4,3},{5,4},{6,5},{7,6},{8,7},{9,8},{10,9},{11,1... | collective-permute-start | bytes 147464 | tf_op jit(solution)/shard_map/ppermute | solution.py:16
  6.2 21.7 %all_gather.3 = bf16[16,64,384]{2,1,0:T(8,128)(2,1)S(1)} all-gather(bf16[1,64,384]{2,1,0:T(8,128)(2,1)} %param.6), channel_id=1, replica_groups=mesh['rep'=2,'walk'=16] {'walk'}, dimensions={0}, use_global_device_ids=true | all-gather | bytes 835584 | tf_op jit(solution)/shard_map/all_gather | solution.py:54
  27.9 68.6 %while.10 = (s32[]{:T(128)}, f32[4,4]{1,0:T(4,128)S(1)}, bf16[4,4,64,384]{3,2,1,0:T(8,128)(2,1)S(1)}, bf16[32,64,384]{2,1,0:T(8,128)(2,1)}, s32[]{:T(128)}, /*index=5*/f32[]{:T(128)}, s32[]{:T(128)}) while((s32[]{:T(128)}, f32[4,4]{1,0:T(4,128)S(1)}, bf16[4,4,64,384]{3,2,1,0:T(8,128)(2,1)S(1)}, bf16[32,64,384]{2,1,0:T(8,128)(2,1)}, s32[]{:T(128)}, ...), condition=%wide.region_3.4_spmd, body=%wide.region_0.3_spmd.sunk | while | flops 403701760 | bytes 44107972 | solution.py:61
  28.0 1.0 broadcast_in_dim.91
  29.4 1.0 broadcast_in_dim.92
  30.4 4.3 %fusion.15 = f32[128,64,64]{2,1,0:T(8,128)} fusion(bf16[128,64,384]{2,1,0:T(8,128)(2,1)S(1)} %bitcast.79, bf16[128,64,384]{2,1,0:T(8,128)(2,1)S(1)} %bitcast.80), kind=kOutput, calls=%fused_computation.41.clone.1 | convolution fusion | flops 402653184 | bytes 14680064 | tf_op jit(solution)/shard_map/while/body/eval_jaxpr/dot_general | solution.py:50
  34.7 5.7 %copy.125 = f32[128,64,64]{1,2,0:T(8,128)} copy(f32[128,64,64]{2,1,0:T(8,128)} %fusion.15) | data formatting | bytes 4194304 | tf_op jit(solution)/shard_map/while/body/eval_jaxpr/dot_general | solution.py:50
  40.4 4.5 %fusion.16 = f32[128]{0:T(128)S(1)} fusion(f32[128,64,64]{2,1,0:T(8,128)} %fusion.15, f32[128,64,64]{1,2,0:T(8,128)} %copy.125), kind=kLoop, calls=%fused_computation.4.clone.1 | loop fusion | flops 1048448 | bytes 4194816 | tf_op jit(solution)/shard_map/while/body/eval_jaxpr/reduce_sum | solution.py:52
  45.2 1.0 broadcast_in_dim.91
  46.5 1.0 broadcast_in_dim.92
  47.6 4.3 %fusion.15 = f32[128,64,64]{2,1,0:T(8,128)} fusion(bf16[128,64,384]{2,1,0:T(8,128)(2,1)S(1)} %bitcast.79, bf16[128,64,384]{2,1,0:T(8,128)(2,1)S(1)} %bitcast.80), kind=kOutput, calls=%fused_computation.41.clone.1 | convolution fusion | flops 402653184 | bytes 14680064 | tf_op jit(solution)/shard_map/while/body/eval_jaxpr/dot_general | solution.py:50
  51.8 5.7 %copy.125 = f32[128,64,64]{1,2,0:T(8,128)} copy(f32[128,64,64]{2,1,0:T(8,128)} %fusion.15) | data formatting | bytes 4194304 | tf_op jit(solution)/shard_map/while/body/eval_jaxpr/dot_general | solution.py:50
  57.5 4.5 %fusion.16 = f32[128]{0:T(128)S(1)} fusion(f32[128,64,64]{2,1,0:T(8,128)} %fusion.15, f32[128,64,64]{1,2,0:T(8,128)} %copy.125), kind=kLoop, calls=%fused_computation.4.clone.1 | loop fusion | flops 1048448 | bytes 4194816 | tf_op jit(solution)/shard_map/while/body/eval_jaxpr/reduce_sum | solution.py:52
  62.3 1.0 broadcast_in_dim.91
  63.7 1.0 broadcast_in_dim.92
  64.7 4.3 %fusion.15 = f32[128,64,64]{2,1,0:T(8,128)} fusion(bf16[128,64,384]{2,1,0:T(8,128)(2,1)S(1)} %bitcast.79, bf16[128,64,384]{2,1,0:T(8,128)(2,1)S(1)} %bitcast.80), kind=kOutput, calls=%fused_computation.41.clone.1 | convolution fusion | flops 402653184 | bytes 14680064 | tf_op jit(solution)/shard_map/while/body/eval_jaxpr/dot_general | solution.py:50
  69.0 5.7 %copy.125 = f32[128,64,64]{1,2,0:T(8,128)} copy(f32[128,64,64]{2,1,0:T(8,128)} %fusion.15) | data formatting | bytes 4194304 | tf_op jit(solution)/shard_map/while/body/eval_jaxpr/dot_general | solution.py:50
  74.7 4.5 %fusion.16 = f32[128]{0:T(128)S(1)} fusion(f32[128,64,64]{2,1,0:T(8,128)} %fusion.15, f32[128,64,64]{1,2,0:T(8,128)} %copy.125), kind=kLoop, calls=%fused_computation.4.clone.1 | loop fusion | flops 1048448 | bytes 4194816 | tf_op jit(solution)/shard_map/while/body/eval_jaxpr/reduce_sum | solution.py:52
  79.5 1.0 broadcast_in_dim.91
  80.8 1.0 broadcast_in_dim.92
  81.9 4.3 %fusion.15 = f32[128,64,64]{2,1,0:T(8,128)} fusion(bf16[128,64,384]{2,1,0:T(8,128)(2,1)S(1)} %bitcast.79, bf16[128,64,384]{2,1,0:T(8,128)(2,1)S(1)} %bitcast.80), kind=kOutput, calls=%fused_computation.41.clone.1 | convolution fusion | flops 402653184 | bytes 14680064 | tf_op jit(solution)/shard_map/while/body/eval_jaxpr/dot_general | solution.py:50
  86.1 5.7 %copy.125 = f32[128,64,64]{1,2,0:T(8,128)} copy(f32[128,64,64]{2,1,0:T(8,128)} %fusion.15) | data formatting | bytes 4194304 | tf_op jit(solution)/shard_map/while/body/eval_jaxpr/dot_general | solution.py:50
  91.8 4.5 %fusion.16 = f32[128]{0:T(128)S(1)} fusion(f32[128,64,64]{2,1,0:T(8,128)} %fusion.15, f32[128,64,64]{1,2,0:T(8,128)} %copy.125), kind=kLoop, calls=%fused_computation.4.clone.1 | loop fusion | flops 1048448 | bytes 4194816 | tf_op jit(solution)/shard_map/while/body/eval_jaxpr/reduce_sum | solution.py:52
  97.4 1.1 constant_dynamic-update-slice_fusion.15
  98.4 1.1 constant_dynamic-update-slice_fusion.14
  99.6 1.1 constant_dynamic-update-slice_fusion.13
  100.7 1.1 constant_dynamic-update-slice_fusion.12
  101.8 1.1 constant_dynamic-update-slice_fusion.11
  102.9 1.1 constant_dynamic-update-slice_fusion.10
  104.1 1.1 constant_dynamic-update-slice_fusion.9
  105.2 1.1 constant_dynamic-update-slice_fusion.8
  106.3 1.1 constant_dynamic-update-slice_fusion.7
  107.5 1.2 constant_dynamic-update-slice_fusion.6
  108.7 1.1 constant_dynamic-update-slice_fusion.5
  109.7 1.2 constant_dynamic-update-slice_fusion.4
  110.9 1.1 constant_dynamic-update-slice_fusion.3
  112.0 1.2 constant_dynamic-update-slice_fusion.2
  113.2 1.2 constant_dynamic-update-slice_fusion.1
  114.3 1.2 constant_dynamic-update-slice_fusion
  115.5 3.5 %all-to-all-start = ((f32[16,1,1]{2,1,0:T(1,128)}), f32[16,1,1]{2,1,0:T(1,128)S(1)}, u32[]{:S(2)}, u32[]{:S(2)}) async-start(f32[16,1,1]{2,1,0:T(1,128)} %constant_dynamic-update-slice_fusion), calls=%async_computation | async-start | bytes 16384 | tf_op jit(solution)/shard_map/all_to_all | solution.py:71
  119.0 3.7 %fusion.1 = f32[16,32,1]{1,0,2:T(8,128)} fusion(bf16[32,64,384]{2,1,0:T(8,128)(2,1)} %get-tuple-element.107, bf16[16,64,384]{2,1,0:T(8,128)(2,1)S(1)} %bitcast.82), kind=kOutput, calls=%fused_computation.7 | convolution fusion | flops 25165824 | bytes 2361344 | tf_op jit(solution)/shard_map/dot_general | solution.py:62
  124.0 1.3 all-to-all-done
  125.3 4.7 %all-to-all-start.1 = ((f32[16,1,32]{2,1,0:T(1,128)}), f32[16,1,32]{2,1,0:T(1,128)S(1)}, u32[]{:S(2)}, u32[]{:S(2)}) async-start(f32[16,1,32]{2,1,0:T(1,128)} %bitcast.26), calls=%async_computation.1 | async-start | bytes 16384 | tf_op jit(solution)/shard_map/all_to_all | solution.py:69
  131.0 4.0 %collective-permute-start.3 = (f32[1]{0:T(128)}, f32[1]{0:T(128)}, u32[]{:S(2)}, u32[]{:S(2)}) collective-permute-start(f32[1]{0:T(128)} %bitcast.23), channel_id=1, source_target_pairs={{1,0},{2,1},{3,2},{4,3},{5,4},{6,5},{7,6},{8,7},{9,8},{10,9},{11,1... | collective-permute-start | bytes 20 | tf_op jit(solution)/shard_map/ppermute | solution.py:16
  135.1 1.5 collective-permute-done.2
  136.5 2.0 %pad_maximum_fusion.2 = f32[3]{0:T(128)S(1)} fusion(f32[1]{0:T(128)} %collective-permute-done.3, f32[1]{0:T(128)} %bitcast.23, f32[1]{0:T(128)} %collective-permute-done.2), kind=kLoop, calls=%fused_computation.37 | loop fusion | flops 6 | bytes 24 | tf_op jit(solution)/shard_map/concatenate | solution.py:17
  140.4 4.5 %collective-permute-start.5 = (f32[1,512]{1,0:T(1,128)S(1)}, f32[1,512]{1,0:T(1,128)S(1)}, u32[]{:S(2)}, u32[]{:S(2)}) collective-permute-start(f32[1,512]{1,0:T(1,128)S(1)} %all_to_all.18), channel_id=1, source_target_pairs={{1,0},{2,1},{3,2},{4,3},{5,4},{6,5},{7,6},{8,7},{9,8},{10,9},{11,1... | collective-permute-start | bytes 6152 | tf_op jit(solution)/shard_map/ppermute | solution.py:16
  144.9 1.2 select_select_fusion.2
  (60 shorter events, 10.7 us)
Async XLA Ops:
  0.6 146.8 %collective-permute-start = (bf16[1,64,384]{2,1,0:T(8,128)(2,1)}, bf16[1,64,384]{2,1,0:T(8,128)(2,1)S(1)}, u32[]{:S(2)}, u32[]{:S(2)}) collective-permute-start(bf16[1,64,384]{2,1,0:T(8,128)(2,1)} %param.6), channel_id=1, source_target_pairs={{0,1},{1,2},{2,3},{3,4},{4,5},{5,6},{6,7},{7,8},{8,9},{9,10},{10,1... | collective-permute-start | bytes 147464 | tf_op jit(solution)/shard_map/ppermute | solution.py:13
  1.1 146.3 %collective-permute-start.1 = (bf16[1,64,384]{2,1,0:T(8,128)(2,1)}, bf16[1,64,384]{2,1,0:T(8,128)(2,1)S(1)}, u32[]{:S(2)}, u32[]{:S(2)}) collective-permute-start(bf16[1,64,384]{2,1,0:T(8,128)(2,1)} %param.6), channel_id=1, source_target_pairs={{1,0},{2,1},{3,2},{4,3},{5,4},{6,5},{7,6},{8,7},{9,8},{10,9},{11,1... | collective-permute-start | bytes 147464 | tf_op jit(solution)/shard_map/ppermute | solution.py:16
  27.9 94.8 %copy-start.3 = (s32[16]{0:T(128)S(1)}, s32[16]{0:T(128)}, u32[]{:S(2)}) copy-start(s32[16]{0:T(128)} %param.8) | copy-start | bytes 196
  27.9 95.4 %copy-start.2 = (s32[2]{0:T(128)S(1)}, s32[2]{0:T(128)}, u32[]{:S(2)}) copy-start(s32[2]{0:T(128)} %param.7) | copy-start | bytes 28
  27.9 119.5 %copy-start.1 = (bf16[1,64,384]{2,1,0:T(8,128)(2,1)S(1)}, bf16[1,64,384]{2,1,0:T(8,128)(2,1)}, u32[]{:S(2)}) copy-start(bf16[1,64,384]{2,1,0:T(8,128)(2,1)} %param.6) | copy-start | bytes 147460
  27.9 1.4 copy-start
  45.1 1.4 copy-start
  62.3 1.4 copy-start
  79.4 1.4 copy-start
  115.5 9.8 %all-to-all-start = ((f32[16,1,1]{2,1,0:T(1,128)}), f32[16,1,1]{2,1,0:T(1,128)S(1)}, u32[]{:S(2)}, u32[]{:S(2)}) async-start(f32[16,1,1]{2,1,0:T(1,128)} %constant_dynamic-update-slice_fusion), calls=%async_computation | async-start | bytes 16384 | tf_op jit(solution)/shard_map/all_to_all | solution.py:71
  125.3 13.9 %all-to-all-start.1 = ((f32[16,1,32]{2,1,0:T(1,128)}), f32[16,1,32]{2,1,0:T(1,128)S(1)}, u32[]{:S(2)}, u32[]{:S(2)}) async-start(f32[16,1,32]{2,1,0:T(1,128)} %bitcast.26), calls=%async_computation.1 | async-start | bytes 16384 | tf_op jit(solution)/shard_map/all_to_all | solution.py:69
  130.6 5.9 %collective-permute-start.2 = (f32[1]{0:T(128)}, f32[1]{0:T(128)}, u32[]{:S(2)}, u32[]{:S(2)}) collective-permute-start(f32[1]{0:T(128)} %bitcast.23), channel_id=1, source_target_pairs={{0,1},{1,2},{2,3},{3,4},{4,5},{5,6},{6,7},{7,8},{8,9},{9,10},{10,1... | collective-permute-start | bytes 20 | tf_op jit(solution)/shard_map/ppermute | solution.py:13
  131.0 5.5 %collective-permute-start.3 = (f32[1]{0:T(128)}, f32[1]{0:T(128)}, u32[]{:S(2)}, u32[]{:S(2)}) collective-permute-start(f32[1]{0:T(128)} %bitcast.23), channel_id=1, source_target_pairs={{1,0},{2,1},{3,2},{4,3},{5,4},{6,5},{7,6},{8,7},{9,8},{10,9},{11,1... | collective-permute-start | bytes 20 | tf_op jit(solution)/shard_map/ppermute | solution.py:16
  140.4 5.7 %collective-permute-start.4 = (f32[1,512]{1,0:T(1,128)S(1)}, f32[1,512]{1,0:T(1,128)S(1)}, u32[]{:S(2)}, u32[]{:S(2)}) collective-permute-start(f32[1,512]{1,0:T(1,128)S(1)} %all_to_all.18), channel_id=1, source_target_pairs={{0,1},{1,2},{2,3},{3,4},{4,5},{5,6},{6,7},{7,8},{8,9},{9,10},{10,1... | collective-permute-start | bytes 6152 | tf_op jit(solution)/shard_map/ppermute | solution.py:13
  140.4 5.8 %collective-permute-start.5 = (f32[1,512]{1,0:T(1,128)S(1)}, f32[1,512]{1,0:T(1,128)S(1)}, u32[]{:S(2)}, u32[]{:S(2)}) collective-permute-start(f32[1,512]{1,0:T(1,128)S(1)} %all_to_all.18), channel_id=1, source_target_pairs={{1,0},{2,1},{3,2},{4,3},{5,4},{6,5},{7,6},{8,7},{9,8},{10,9},{11,1... | collective-permute-start | bytes 6152 | tf_op jit(solution)/shard_map/ppermute | solution.py:16
